TPU v7x, 32 devices: a whole 2x2x4 slice. The times are simulated.
32 devices in a mesh: row: 4 (over y, x), col: 8 (over z, core).
Axes of the slice: x: 2, y: 2, z: 4, core: 2. Of those that a mesh axis runs over, the one named last changes fastest.
Arguments:
- velocities: bfloat16 [1024, 30720], P(None, 'row'), may hold values from -60 to 60, as said below
- modes_panel: bfloat16 [30720, 4096], P('row', 'col'), may hold values from -1 to 1
- atom_slot: int32 [10240], P('row'), may hold values from 0 to 2559, as said below
- lag_offsets: int32 [8], replicated, may hold values from 0 to 256, as said below
Outputs:
- correlations: float32 [8, 4096, 4096], P(None, 'row', 'col')
Inputs may be any that keep to these rules, and one draw needn't show every extreme that they name: `velocities`: every snapshot row has its own scale. Within each aligned block of 2560 atoms, atom_slot is a permutation of 0 to 2559. `lag_offsets`: one of the lags equals 256.
All inputs are finite; a program needn't handle non-finite values.
Results may differ from a plain program's by a relative error of at most 0.0041.
Values may be sent and summed in bfloat16 or wider, within the bound.
No kernel may reach another device: no remote copies, remote signals or barrier semaphores. Data moves between devices by JAX's collectives and lax.ppermute only.
A program may use at most 128 MiB of HBM per device.

v0:
```python
import functools

import jax
import jax.numpy as jnp
from jax import lax
from jax.experimental import pallas as pl
from jax.experimental.pallas import tpu as pltpu
from jax.sharding import PartitionSpec as P


MAXLAG = 256
LANES = 128
ROWS = 8
GROUP = 16
MARGIN = 3 << 20

epsilon = 1e-06


def swap(block, axis, offset):
    size = lax.axis_size(axis)
    return lax.ppermute(block, axis, [(i, i ^ offset) for i in range(size)])


def reorder_chunk(slot, source, ordered, chunk, c):
    blocks = source.shape[0]
    row = lax.broadcasted_iota(jnp.int32, (ROWS, LANES), 0)
    groups = chunk // (3 * GROUP)

    def move(g, carry):
        g = c * groups + g
        base = [slot[g * GROUP + i] for i in range(GROUP)]
        for j in range(blocks):
            tiles = []
            for v in range(3 * GROUP // ROWS):
                tile = None
                for i in range(GROUP):
                    low = 3 * i - ROWS * v
                    if low + 3 <= 0 or low >= ROWS:
                        continue
                    piece = source[j, pl.ds(base[i] + (ROWS - low), ROWS), :]
                    tile = piece if tile is None else jnp.where(row >= low, piece, tile)
                tiles.append(tile)
            ordered[
                pl.ds(pl.multiple_of(g * 3 * GROUP, GROUP), 3 * GROUP), j * LANES : (j + 1) * LANES
            ] = jnp.concatenate(tiles, axis=0).astype(jnp.bfloat16)
        return carry

    lax.fori_loop(0, groups, move, 0, unroll=8)


def arrangement(lists):
    left, right = lists
    order = [m for m in left if m not in right] + [m for m in left if m in right]
    order += [m for m in right if m not in left]
    runs = [(min(order.index(m) for m in held), len(held)) for held in lists]
    return order, runs


def row_starts(order, size):
    mine = lax.axis_index("row")
    return [pl.multiple_of((mine ^ m) * size, size) for m in order]


def add_products(total, rows, part, ordered, runs, size):
    half = ordered.shape[1] // 2
    for h, (first, count) in enumerate(runs):
        columns = slice(h * half, (h + 1) * half)
        total[: count * size, columns] += jnp.dot(
            rows[first * size : (first + count) * size, part],
            ordered[part, columns],
            preferred_element_type=jnp.float32,
        )


def write_turned(total, outs):
    half, size = outs[0].shape
    count = len(outs) // 2
    for h in range(2):
        for i in range(count):
            outs[h * count + i][...] = total[i * size : (i + 1) * size, h * half : (h + 1) * half].T


def reorder_project_kernel(slot, panel, velocities, *refs, chunk, order, runs):
    count = runs[0][1]
    outs, ordered_out = refs[: 2 * count], refs[2 * count]
    tripled, slots, staged, source, rows, total, slot_sem, in_sems, row_sems, out_sem = refs[2 * count + 1 :]
    depth, width = panel.shape
    blocks = width // LANES
    size = outs[0].shape[1]
    chunks = depth // chunk
    starts = row_starts(order, size)

    def panel_copy(c):
        part = pl.ds(c * chunk, chunk)
        return pltpu.make_async_copy(panel.at[part, :], staged.at[part, :], in_sems.at[c])

    def row_copy(i, c):
        part = pl.ds(pl.multiple_of(c * chunk, chunk), chunk)
        return pltpu.make_async_copy(
            velocities.at[pl.ds(starts[i], size), part],
            rows.at[pl.ds(i * size, size), part],
            row_sems.at[c, i],
        )

    def ordered_copy(c):
        part = pl.ds(pl.multiple_of(c * chunk, chunk), chunk)
        return pltpu.make_async_copy(staged.at[part, :], ordered_out.at[part, :], out_sem)

    first_copy = pltpu.make_async_copy(slot, tripled, slot_sem)
    first_copy.start()
    for c in range(chunks):
        panel_copy(c).start()
    for c in range(chunks):
        for i in range(len(order)):
            row_copy(i, c).start()
    first_copy.wait()
    tripled[...] = tripled[...] * 3
    slot_copy = pltpu.make_async_copy(tripled, slots, slot_sem)
    slot_copy.start()
    total[...] = jnp.zeros_like(total)
    for c in range(chunks):
        panel_copy(c).wait()

        def widen(i, carry):
            first = pl.multiple_of(c * chunk + i * LANES, LANES)
            for j in range(blocks):
                source[j, pl.ds(ROWS + first, LANES), :] = staged[
                    pl.ds(first, LANES), j * LANES : (j + 1) * LANES
                ].astype(jnp.float32)
            return carry

        lax.fori_loop(0, chunk // LANES, widen, 0)
    slot_copy.wait()

    def body(c, carry):
        reorder_chunk(slots, source, staged, chunk, c)
        ordered_copy(c).start()
        for i in range(len(order)):
            row_copy(i, c).wait()
        part = pl.ds(pl.multiple_of(c * chunk, chunk), chunk)
        add_products(total, rows, part, staged, runs, size)
        return carry

    lax.fori_loop(0, chunks, body, 0)
    write_turned(total, outs)
    for c in range(chunks):
        ordered_copy(c).wait()


def reorder_project(panel, velocities, slot, lists, size):
    depth, width = panel.shape
    order, runs = arrangement(lists)
    count = runs[0][1]
    chunk = depth // 10
    anywhere = pl.BlockSpec(memory_space=pl.ANY)
    part = jax.ShapeDtypeStruct((width // 2, size), jnp.float32)
    *parts, ordered = pl.pallas_call(
        functools.partial(reorder_project_kernel, chunk=chunk, order=order, runs=runs),
        out_shape=[part] * (2 * count) + [jax.ShapeDtypeStruct((depth, width), jnp.bfloat16)],
        grid=(1,),
        in_specs=[pl.BlockSpec(memory_space=pltpu.HBM)] * 3,
        out_specs=[pl.BlockSpec((width // 2, size), lambda i: (0, 0))] * (2 * count) + [anywhere],
        scratch_shapes=[
            pltpu.VMEM(slot.shape, jnp.int32),
            pltpu.SMEM(slot.shape, jnp.int32),
            pltpu.VMEM((depth, width), jnp.bfloat16),
            pltpu.VMEM((width // LANES, depth + 2 * ROWS, LANES), jnp.float32),
            pltpu.VMEM((len(order) * size, depth), jnp.bfloat16),
            pltpu.VMEM((count * size, width), jnp.float32),
            pltpu.SemaphoreType.DMA,
            pltpu.SemaphoreType.DMA((depth // chunk,)),
            pltpu.SemaphoreType.DMA((depth // chunk, len(order))),
            pltpu.SemaphoreType.DMA,
        ],
        cost_estimate=pl.CostEstimate(
            flops=2 * count * size * depth * width,
            bytes_accessed=2 * depth * (2 * width + count * size),
            transcendentals=0,
        ),
        compiler_params=pltpu.CompilerParams(
            vmem_limit_bytes=2 * depth * (3 * width + len(order) * size) + 4 * size * width * count * 3 + MARGIN
        ),
        name="reorder_project",
    )(*(pltpu.with_memory_space_constraint(x, pltpu.HBM) for x in (slot, panel, velocities)))
    return parts_by_piece(parts, order, runs), ordered


def parts_by_piece(parts, order, runs):
    return [
        {m: parts[h * count + i] for i, m in enumerate(order[first : first + count])}
        for h, (first, count) in enumerate(runs)
    ]


def project_kernel(panel, velocities, *refs, chunk, order, runs):
    count = runs[0][1]
    outs = refs[: 2 * count]
    staged, rows, total, sems = refs[2 * count :]
    depth = panel.shape[0]
    size = outs[0].shape[1]
    chunks = depth // chunk
    starts = row_starts(order, size)

    def copies(c):
        part = pl.ds(c * chunk, chunk)
        yield pltpu.make_async_copy(panel.at[part, :], staged.at[part, :], sems.at[c, len(order)])
        for i, start in enumerate(starts):
            yield pltpu.make_async_copy(
                velocities.at[pl.ds(start, size), part], rows.at[pl.ds(i * size, size), part], sems.at[c, i]
            )

    for c in range(chunks):
        for copy in copies(c):
            copy.start()
    total[...] = jnp.zeros_like(total)
    for c in range(chunks):
        for copy in copies(c):
            copy.wait()
        add_products(total, rows, slice(c * chunk, (c + 1) * chunk), staged, runs, size)
    write_turned(total, outs)


def project(ordered, velocities, lists, size):
    depth, width = ordered.shape
    order, runs = arrangement(lists)
    count = runs[0][1]
    chunk = depth // 10
    anywhere = pl.BlockSpec(memory_space=pl.ANY)
    parts = pl.pallas_call(
        functools.partial(project_kernel, chunk=chunk, order=order, runs=runs),
        out_shape=[jax.ShapeDtypeStruct((width // 2, size), jnp.float32)] * (2 * count),
        grid=(1,),
        in_specs=[anywhere, pl.BlockSpec(memory_space=pltpu.HBM)],
        out_specs=[pl.BlockSpec((width // 2, size), lambda i: (0, 0))] * (2 * count),
        scratch_shapes=[
            pltpu.VMEM((depth, width), jnp.bfloat16),
            pltpu.VMEM((len(order) * size, depth), jnp.bfloat16),
            pltpu.VMEM((count * size, width), jnp.float32),
            pltpu.SemaphoreType.DMA((depth // chunk, len(order) + 1)),
        ],
        cost_estimate=pl.CostEstimate(
            flops=2 * count * size * depth * width,
            bytes_accessed=2 * depth * (width + len(order) * size),
            transcendentals=0,
        ),
        compiler_params=pltpu.CompilerParams(
            vmem_limit_bytes=2 * depth * (width + len(order) * size) + 4 * size * width * count * 3 + MARGIN
        ),
        name="project",
    )(ordered, pltpu.with_memory_space_constraint(velocities, pltpu.HBM))
    return parts_by_piece(parts, order, runs)


def shift_kernel(offsets, *refs, parts):
    pieces, out, source = refs[:parts], refs[parts], refs[parts + 1]
    blocks, length, _ = source.shape
    size = pieces[0].shape[1]
    snapshots = parts * size

    @pl.when(pl.program_id(0) == 0)
    def _():
        for j in range(blocks):
            columns = slice(j * LANES, (j + 1) * LANES)
            for m, piece in enumerate(pieces):
                start = pl.multiple_of((lax.axis_index("row") ^ m) * size, size)
                source[j, pl.ds(start, size), :] = piece[columns, :].astype(jnp.float32).T
            source[j, snapshots:, :] = jnp.zeros((length - snapshots, LANES), jnp.float32)

    offset = offsets[pl.program_id(0)]
    step = 128

    def body(i, carry):
        first = pl.multiple_of(i * step, step)
        for j in range(blocks):
            out[0, pl.ds(first, step), j * LANES : (j + 1) * LANES] = source[
                j, pl.ds(first + offset, step), :
            ].astype(jnp.bfloat16)
        return carry

    lax.fori_loop(0, snapshots // step, body, 0)


def shifted_copies(pieces, lag_offsets):
    width, size = pieces[0].shape
    parts = len(pieces)
    snapshots = size * parts
    lags = lag_offsets.shape[0]
    whole = pl.BlockSpec((width, size), lambda l, s: (0, 0))
    return pl.pallas_call(
        functools.partial(shift_kernel, parts=parts),
        out_shape=jax.ShapeDtypeStruct((lags, snapshots, width), jnp.bfloat16),
        grid_spec=pltpu.PrefetchScalarGridSpec(
            num_scalar_prefetch=1,
            grid=(lags,),
            in_specs=[whole] * parts,
            out_specs=pl.BlockSpec((1, snapshots, width), lambda l, s: (l, 0, 0)),
            scratch_shapes=[pltpu.VMEM((width // LANES, snapshots + MAXLAG + ROWS, LANES), jnp.float32)],
        ),
        cost_estimate=pl.CostEstimate(
            flops=0, bytes_accessed=2 * snapshots * width * (lags + 1), transcendentals=0
        ),
        compiler_params=pltpu.CompilerParams(
            vmem_limit_bytes=4 * width * (snapshots + MAXLAG) + 8 * snapshots * width + MARGIN
        ),
        name="shift",
    )(lag_offsets, *pieces)


def correlate_kernel(factors, *refs, parts, owners, half):
    mine, others = refs[:parts], refs[parts : parts + owners - 1]
    shifted = refs[parts + owners - 1]
    out, turned, lagged, results, in_sems, lag_sems, out_sems = refs[-7:]
    lags = shifted.shape[0]
    modes, size = mine[0].shape
    row = lax.axis_index("row")
    member = lax.rem(lax.axis_index("col"), owners)
    copies = []
    for m in range(parts):
        place = pl.ds(pl.multiple_of((row ^ m) * size, size), size)
        for k in range(owners):
            piece = mine[m] if k == 0 else others[k - 1].at[m]
            copies.append(
                pltpu.make_async_copy(piece, turned.at[pl.ds(k * modes, modes), place], in_sems.at[m, k])
            )
    for copy in copies:
        copy.start()

    def lag_copy(l):
        return pltpu.make_async_copy(shifted.at[l], lagged.at[l], lag_sems.at[l])

    def out_copies(l):
        for k in range(owners):
            first = ((member ^ k) * 2 + half) * modes
            yield pltpu.make_async_copy(
                results.at[l, pl.ds(k * modes, modes), :],
                out.at[l, pl.ds(pl.multiple_of(first, modes), modes), :],
                out_sems.at[l, k],
            )

    for l in range(lags):
        lag_copy(l).start()
    for copy in copies:
        copy.wait()

    def body(l, carry):
        lag_copy(l).wait()
        product = jnp.dot(turned[...], lagged[l], preferred_element_type=jnp.float32)
        results[l] = product * factors[l]
        for copy in out_copies(l):
            copy.start()
        return carry

    lax.fori_loop(0, lags, body, 0)
    for l in range(lags):
        for copy in out_copies(l):
            copy.wait()


def correlate(mine, others, shifted, factors, half, out_shape, previous):
    modes, _ = mine[0].shape
    parts, owners = len(mine), len(others) + 1
    lags, snapshots, width = shifted.shape
    operands = [*mine, *others, shifted]
    aliases = {}
    if previous is not None:
        aliases = {len(operands) + 1: 0}
        operands.append(previous)
    anywhere = pl.BlockSpec(memory_space=pl.ANY)
    return pl.pallas_call(
        functools.partial(correlate_kernel, parts=parts, owners=owners, half=half),
        out_shape=jax.ShapeDtypeStruct(out_shape, jnp.float32),
        grid_spec=pltpu.PrefetchScalarGridSpec(
            num_scalar_prefetch=1,
            grid=(1,),
            in_specs=[anywhere] * len(operands),
            out_specs=anywhere,
            scratch_shapes=[
                pltpu.VMEM((owners * modes, snapshots), jnp.bfloat16),
                pltpu.VMEM((lags, snapshots, width), jnp.bfloat16),
                pltpu.VMEM((lags, owners * modes, width), jnp.float32),
                pltpu.SemaphoreType.DMA((parts, owners)),
                pltpu.SemaphoreType.DMA((lags,)),
                pltpu.SemaphoreType.DMA((lags, owners)),
            ],
        ),
        input_output_aliases=aliases,
        cost_estimate=pl.CostEstimate(
            flops=2 * lags * owners * modes * snapshots * width,
            bytes_accessed=lags * width * (2 * snapshots + 4 * owners * modes),
            transcendentals=0,
        ),
        compiler_params=pltpu.CompilerParams(
            vmem_limit_bytes=lags * width * (2 * snapshots + 4 * owners * modes)
            + 2 * owners * modes * snapshots
            + MARGIN
        ),
        name="correlate",
    )(factors, *operands)


def reduce_scatter(held, bits):
    live = range(len(held))
    held = dict(held)
    for bit in bits:
        for m in reversed(live):
            if m & bit:
                arrived = swap(held[m], "row", bit)
                held[m ^ bit] = held[m ^ bit] + arrived
        live = [m for m in live if not m & bit]
    return held[0]


def steps(velocities, modes_panel, atom_slot, lag_offsets):
    ranks = lax.axis_size("row")
    columns = lax.axis_size("col")
    owners = columns // ranks
    mine = lax.axis_index("row")
    group = lax.axis_index("col") // owners
    snapshots = velocities.shape[0]
    size = snapshots // ranks
    width = modes_panel.shape[1]
    modes = width * columns

    bits = [1 << b for b in range(ranks.bit_length() - 1)]
    orders = [bits, bits[::-1]]
    early = [[m for m in range(ranks) if m & order[0]] for order in orders]
    late = [[m for m in range(ranks) if not m & order[0]] for order in orders]
    early_parts, ordered = reorder_project(modes_panel, velocities, atom_slot, early, size)
    late_parts = project(ordered, velocities, late, size)
    halves = [reduce_scatter(early_parts[h] | late_parts[h], orders[h]) for h in range(2)]

    energy = sum(jnp.sum(half * half, axis=0) for half in halves)
    bit = 1
    while bit < columns:
        energy = energy + swap(energy, "col", bit)
        bit *= 2
    scale = lax.rsqrt(energy / modes + epsilon)[None, :]
    halves = [(half * scale).astype(jnp.bfloat16) for half in halves]
    own = jnp.concatenate(halves, axis=0)

    across = []
    for h in range(2):
        across.append([halves[h]] + [swap(halves[h], "col", owners * m) for m in range(1, ranks)])
    column_pieces = [own] + [swap(own, "row", m) for m in range(1, ranks)]
    shifted = shifted_copies(column_pieces, lag_offsets)

    factors = lax.rsqrt((snapshots - lag_offsets).astype(jnp.float32))
    out_shape = (lag_offsets.shape[0], width * owners, width)
    result = None
    for h in range(2):
        if h == 1:
            across[h], shifted = lax.optimization_barrier((across[h], shifted))
        stacked = jnp.stack(across[h])
        pieces = []
        for m in range(ranks):
            chosen = lax.dynamic_index_in_dim(stacked, group ^ mine ^ m, 0, keepdims=False)
            if m:
                chosen = swap(chosen, "row", m)
            pieces.append(chosen)
        if h == 1:
            pieces, result = lax.optimization_barrier((pieces, result))
        joined = jnp.stack(pieces)
        others = [swap(joined, "col", k) for k in range(1, owners)]
        result = correlate(pieces, others, shifted, factors, h, out_shape, result)
    return result


def solution(mesh):
    return jax.shard_map(
        steps,
        mesh=mesh,
        in_specs=(P(None, "row"), P("row", "col"), P("row"), P()),
        out_specs=P(None, "row", "col"),
        check_vma=False,
    )
```

profile of v0, /device:TPU:0, one launch (start us, length us, event | category | flops | bytes accessed | tf_op | source)
XLA Modules:
  0.0 122.5 jit_solution(524363314777926090)
XLA Ops:
  0.0 20.5 %reorder_project.1 = (f32[256,256]{1,0:T(8,128)S(1)}, f32[256,256]{1,0:T(8,128)S(1)}, f32[256,256]{1,0:T(8,128)S(1)}, f32[256,256]{1,0:T(8,128)S(1)}, bf16[7680,512]{1,0:T(8,128)(2,1)S(1)}) custom-call(s32[2560]{0:T(1024)} %slot.1, bf16[7680,512]{1,0:T(8,128)(2,1)} %panel.1, bf16[1024,7680]{1,0:T(8,128)(2,1)} %velocities.3), custom_call_target="tpu_custom_call" | custom-call | flops 4026531840 | bytes 23592960 | tf_op jit(solution)/shard_map/reorder_project/pallas_call | solution.py:158
  20.6 3.1 %collective-permute-start = (f32[256,256]{1,0:T(8,128)S(1)}, f32[256,256]{1,0:T(8,128)S(1)}, u32[]{:S(2)}, u32[]{:S(2)}) collective-permute-start(f32[256,256]{1,0:T(8,128)S(1)} %get-tuple-element.26), channel_id=1, source_target_pairs={{0,16},{8,24},{16,0},{24,8},{1,17},{9,25},{17,1},{25,9},{2,18},{10... | collective-permute-start | bytes 786440 | tf_op jit(solution)/shard_map/ppermute | solution.py:22
  23.6 0.1 collective-permute-start.1
  23.7 1.9 %collective-permute-start.4 = (f32[256,256]{1,0:T(8,128)S(1)}, f32[256,256]{1,0:T(8,128)S(1)}, u32[]{:S(2)}, u32[]{:S(2)}) collective-permute-start(f32[256,256]{1,0:T(8,128)S(1)} %get-tuple-element.32), channel_id=1, source_target_pairs={{0,8},{8,0},{16,24},{24,16},{1,9},{9,1},{17,25},{25,17},{2,10},{10... | collective-permute-start | bytes 786440 | tf_op jit(solution)/shard_map/ppermute | solution.py:22
  25.6 6.6 %project.1 = (f32[256,256]{1,0:T(8,128)S(1)}, f32[256,256]{1,0:T(8,128)S(1)}, f32[256,256]{1,0:T(8,128)S(1)}, f32[256,256]{1,0:T(8,128)S(1)}) custom-call(bf16[7680,512]{1,0:T(8,128)(2,1)S(1)} %get-tuple-element.24.panel, bf16[1024,7680]{1,0:T(8,128)(2,1)} %velocities.3), custom_call_target="tpu_custom_call" | custom-call | flops 4026531840 | bytes 19660800 | tf_op jit(solution)/shard_map/project/pallas_call | solution.py:230
  32.2 3.3 %collective-permute-done.1 = f32[256,256]{1,0:T(8,128)S(1)} collective-permute-done((f32[256,256]{1,0:T(8,128)S(1)}, f32[256,256]{1,0:T(8,128)S(1)}, u32[]{:S(2)}, u32[]{:S(2)}) %collective-permute-start.1) | collective-permute-done | bytes 262176 | tf_op jit(solution)/shard_map/ppermute | solution.py:22
  35.6 1.8 %collective-permute-start.2 = (f32[256,256]{1,0:T(8,128)S(1)}, f32[256,256]{1,0:T(8,128)S(1)}, u32[]{:S(2)}, u32[]{:S(2)}) collective-permute-start(f32[256,256]{1,0:T(8,128)S(1)} %add.55), channel_id=1, source_target_pairs={{0,8},{8,0},{16,24},{24,16},{1,9},{9,1},{17,25},{25,17},{2,10},{10... | collective-permute-start | bytes 786440 | tf_op jit(solution)/shard_map/ppermute | solution.py:22
  37.3 0.3 collective-permute-start.3
  37.7 0.0 collective-permute-done.4
  37.7 1.8 %collective-permute-start.5 = (f32[256,256]{1,0:T(8,128)S(1)}, f32[256,256]{1,0:T(8,128)S(1)}, u32[]{:S(2)}, u32[]{:S(2)}) collective-permute-start(f32[256,256]{1,0:T(8,128)S(1)} %add.58), channel_id=1, source_target_pairs={{0,16},{8,24},{16,0},{24,8},{1,17},{9,25},{17,1},{25,9},{2,18},{10... | collective-permute-start | bytes 786440 | tf_op jit(solution)/shard_map/ppermute | solution.py:22
  39.5 0.0 collective-permute-done
  39.5 5.3 %collective-permute-done.2 = f32[256,256]{1,0:T(8,128)S(1)} collective-permute-done((f32[256,256]{1,0:T(8,128)S(1)}, f32[256,256]{1,0:T(8,128)S(1)}, u32[]{:S(2)}, u32[]{:S(2)}) %collective-permute-start.2) | collective-permute-done | bytes 262176 | tf_op jit(solution)/shard_map/ppermute | solution.py:22
  44.8 0.1 multiply_reduce_fusion
  44.9 3.8 %collective-permute-done.3 = f32[256,256]{1,0:T(8,128)S(1)} collective-permute-done((f32[256,256]{1,0:T(8,128)S(1)}, f32[256,256]{1,0:T(8,128)S(1)}, u32[]{:S(2)}, u32[]{:S(2)}) %collective-permute-start.3) | collective-permute-done | bytes 262176 | tf_op jit(solution)/shard_map/ppermute | solution.py:22
  48.7 0.0 collective-permute-done.5
  48.7 0.1 multiply_reduce_fusion.1
  48.8 0.1 collective-permute-start.6
  48.9 1.1 collective-permute-done.6
  50.0 1.5 %collective-permute-start.7 = (f32[256]{0:T(256)S(1)}, f32[256]{0:T(256)S(1)}, u32[]{:S(2)}, u32[]{:S(2)}) collective-permute-start(f32[256]{0:T(256)S(1)} %add.61), channel_id=1, source_target_pairs={{0,2},{1,3},{2,0},{3,1},{4,6},{5,7},{6,4},{7,5},{8,10},{9,11},{10,... | collective-permute-start | bytes 3080 | tf_op jit(solution)/shard_map/ppermute | solution.py:22
  51.6 2.0 %collective-permute-done.7 = f32[256]{0:T(256)S(1)} collective-permute-done((f32[256]{0:T(256)S(1)}, f32[256]{0:T(256)S(1)}, u32[]{:S(2)}, u32[]{:S(2)}) %collective-permute-start.7) | collective-permute-done | bytes 1056 | tf_op jit(solution)/shard_map/ppermute | solution.py:22
  53.6 2.5 %collective-permute-start.8 = (f32[256]{0:T(256)S(1)}, f32[256]{0:T(256)S(1)}, u32[]{:S(2)}, u32[]{:S(2)}) collective-permute-start(f32[256]{0:T(256)S(1)} %add.62), channel_id=1, source_target_pairs={{0,4},{1,5},{2,6},{3,7},{4,0},{5,1},{6,2},{7,3},{8,12},{9,13},{10,... | collective-permute-start | bytes 3080 | tf_op jit(solution)/shard_map/ppermute | solution.py:22
  56.1 2.0 %collective-permute-done.8 = f32[256]{0:T(256)S(1)} collective-permute-done((f32[256]{0:T(256)S(1)}, f32[256]{0:T(256)S(1)}, u32[]{:S(2)}, u32[]{:S(2)}) %collective-permute-start.8) | collective-permute-done | bytes 1056 | tf_op jit(solution)/shard_map/ppermute | solution.py:22
  58.1 0.1 multiply_convert_fusion
  58.2 3.6 %collective-permute-start.20 = (bf16[256,256]{1,0:T(8,128)(2,1)S(1)}, bf16[256,256]{1,0:T(8,128)(2,1)S(1)}, u32[]{:S(2)}, u32[]{:S(2)}) collective-permute-start(bf16[256,256]{1,0:T(8,128)(2,1)S(1)} %get-tuple-element.51), channel_id=1, source_target_pairs={{0,6},{1,7},{2,4},{3,5},{4,2},{5,3},{6,0},{7,1},{8,14},{9,15},{10,... | collective-permute-start | bytes 393224 | tf_op jit(solution)/shard_map/ppermute | solution.py:22
  61.8 0.0 collective-permute-start.19
  61.8 0.8 collective-permute-start.18
  62.7 3.3 %collective-permute-done.20 = bf16[256,256]{1,0:T(8,128)(2,1)S(1)} collective-permute-done((bf16[256,256]{1,0:T(8,128)(2,1)S(1)}, bf16[256,256]{1,0:T(8,128)(2,1)S(1)}, u32[]{:S(2)}, u32[]{:S(2)}) %collective-permute-start.20) | collective-permute-done | bytes 131104 | tf_op jit(solution)/shard_map/ppermute | solution.py:22
  66.0 4.9 %collective-permute-done.19 = bf16[256,256]{1,0:T(8,128)(2,1)S(1)} collective-permute-done((bf16[256,256]{1,0:T(8,128)(2,1)S(1)}, bf16[256,256]{1,0:T(8,128)(2,1)S(1)}, u32[]{:S(2)}, u32[]{:S(2)}) %collective-permute-start.19) | collective-permute-done | bytes 131104 | tf_op jit(solution)/shard_map/ppermute | solution.py:22
  70.9 0.0 collective-permute-done.18
  70.9 0.1 pad_maximum_fusion.1
  71.1 2.5 %collective-permute-start.23 = (bf16[256,256]{1,0:T(8,128)(2,1)S(1)}, bf16[256,256]{1,0:T(8,128)(2,1)S(1)}, u32[]{:S(2)}, u32[]{:S(2)}) collective-permute-start(bf16[256,256]{1,0:T(8,128)(2,1)S(1)} %get-tuple-element.43), channel_id=1, source_target_pairs={{0,24},{8,16},{16,8},{24,0},{1,25},{9,17},{17,9},{25,1},{2,26},{10... | collective-permute-start | bytes 393224 | tf_op jit(solution)/shard_map/ppermute | solution.py:22
  73.6 0.5 collective-permute-start.22
  74.1 0.6 collective-permute-start.21
  74.7 2.5 %collective-permute-start.14 = (bf16[512,256]{1,0:T(8,128)(2,1)S(1)}, bf16[512,256]{1,0:T(8,128)(2,1)S(1)}, u32[]{:S(2)}, u32[]{:S(2)}) collective-permute-start(bf16[512,256]{1,0:T(8,128)(2,1)S(1)} %pad_maximum_fusion.4.refs_0_), channel_id=1, source_target_pairs={{0,24},{8,16},{16,8},{24,0},{1,25},{9,17},{17,9},{25,1},{2,26},{10... | collective-permute-start | bytes 786440 | tf_op jit(solution)/shard_map/ppermute | solution.py:22
  77.2 0.5 collective-permute-start.13
  77.6 0.1 collective-permute-done.23.refs_3_
  77.7 8.1 %collective-permute-done.22.refs_2_ = bf16[256,256]{1,0:T(8,128)(2,1)S(1)} collective-permute-done((bf16[256,256]{1,0:T(8,128)(2,1)S(1)}, bf16[256,256]{1,0:T(8,128)(2,1)S(1)}, u32[]{:S(2)}, u32[]{:S(2)}) %collective-permute-start.22) | collective-permute-done | bytes 131104 | tf_op jit(solution)/shard_map/ppermute | solution.py:22
  85.9 0.0 collective-permute-done.21.refs_1_
  85.9 0.1 pad_maximum_fusion.2
  85.9 0.1 collective-permute-start.24
  86.0 1.4 %collective-permute-start.12 = (bf16[512,256]{1,0:T(8,128)(2,1)S(1)}, bf16[512,256]{1,0:T(8,128)(2,1)S(1)}, u32[]{:S(2)}, u32[]{:S(2)}) collective-permute-start(bf16[512,256]{1,0:T(8,128)(2,1)S(1)} %pad_maximum_fusion.4.refs_0_), channel_id=1, source_target_pairs={{0,8},{8,0},{16,24},{24,16},{1,9},{9,1},{17,25},{25,17},{2,10},{10... | collective-permute-start | bytes 786440 | tf_op jit(solution)/shard_map/ppermute | solution.py:22
  87.4 2.0 %collective-permute-start.11 = (bf16[256,256]{1,0:T(8,128)(2,1)S(1)}, bf16[256,256]{1,0:T(8,128)(2,1)S(1)}, u32[]{:S(2)}, u32[]{:S(2)}) collective-permute-start(bf16[256,256]{1,0:T(8,128)(2,1)S(1)} %get-tuple-element.33), channel_id=1, source_target_pairs={{0,6},{1,7},{2,4},{3,5},{4,2},{5,3},{6,0},{7,1},{8,14},{9,15},{10,... | collective-permute-start | bytes 393224 | tf_op jit(solution)/shard_map/ppermute | solution.py:22
  89.4 0.0 collective-permute-done.14.refs_3_
  89.4 0.0 collective-permute-start.10
  89.4 1.3 %collective-permute-done.13.refs_2_ = bf16[512,256]{1,0:T(8,128)(2,1)S(1)} collective-permute-done((bf16[512,256]{1,0:T(8,128)(2,1)S(1)}, bf16[512,256]{1,0:T(8,128)(2,1)S(1)}, u32[]{:S(2)}, u32[]{:S(2)}) %collective-permute-start.13) | collective-permute-done | bytes 262176 | tf_op jit(solution)/shard_map/ppermute | solution.py:22
  90.7 1.1 collective-permute-start.9
  91.8 2.9 %collective-permute-done.12.refs_1_ = bf16[512,256]{1,0:T(8,128)(2,1)S(1)} collective-permute-done((bf16[512,256]{1,0:T(8,128)(2,1)S(1)}, bf16[512,256]{1,0:T(8,128)(2,1)S(1)}, u32[]{:S(2)}, u32[]{:S(2)}) %collective-permute-start.12) | collective-permute-done | bytes 262176 | tf_op jit(solution)/shard_map/ppermute | solution.py:22
  94.7 2.5 %shift.1.refs_5_ = bf16[8,1024,512]{2,1,0:T(8,128)(2,1)S(1)} custom-call(s32[8]{0:T(128)S(1)} %copy-done, bf16[512,256]{1,0:T(8,128)(2,1)S(1)} %pad_maximum_fusion.4.refs_0_, bf16[512,256]{1,0:T(8,128)(2,1)S(1)} %collective-permute-done.12.refs_1_, bf16[512,256]{1,0:T(8,128)(2,1)S(1)} %collective-permute-done.13.refs_2_, ...), custom_call_target="tpu_custom_call" | custom-call | bytes 9437184 | tf_op jit(solution)/shard_map/shift/pallas_call | solution.py:290
  97.2 0.0 collective-permute-done.11
  97.2 3.2 %collective-permute-done.10 = bf16[256,256]{1,0:T(8,128)(2,1)S(1)} collective-permute-done((bf16[256,256]{1,0:T(8,128)(2,1)S(1)}, bf16[256,256]{1,0:T(8,128)(2,1)S(1)}, u32[]{:S(2)}, u32[]{:S(2)}) %collective-permute-start.10) | collective-permute-done | bytes 131104 | tf_op jit(solution)/shard_map/ppermute | solution.py:22
  100.4 0.0 collective-permute-done.9
  100.4 0.1 pad_maximum_fusion
  100.5 1.5 %collective-permute-start.17 = (bf16[256,256]{1,0:T(8,128)(2,1)S(1)}, bf16[256,256]{1,0:T(8,128)(2,1)S(1)}, u32[]{:S(2)}, u32[]{:S(2)}) collective-permute-start(bf16[256,256]{1,0:T(8,128)(2,1)S(1)} %get-tuple-element.47), channel_id=1, source_target_pairs={{0,24},{8,16},{16,8},{24,0},{1,25},{9,17},{17,9},{25,1},{2,26},{10... | collective-permute-start | bytes 393224 | tf_op jit(solution)/shard_map/ppermute | solution.py:22
  102.0 0.7 collective-permute-start.16
  102.7 1.3 %collective-permute-start.15 = (bf16[256,256]{1,0:T(8,128)(2,1)S(1)}, bf16[256,256]{1,0:T(8,128)(2,1)S(1)}, u32[]{:S(2)}, u32[]{:S(2)}) collective-permute-start(bf16[256,256]{1,0:T(8,128)(2,1)S(1)} %get-tuple-element.49), channel_id=1, source_target_pairs={{0,8},{8,0},{16,24},{24,16},{1,9},{9,1},{17,25},{25,17},{2,10},{10... | collective-permute-start | bytes 393224 | tf_op jit(solution)/shard_map/ppermute | solution.py:22
  104.1 0.0 collective-permute-done.24.refs_4_
  104.1 8.2 %correlate.2.refs_6_ = f32[8,1024,512]{2,1,0:T(8,128)} custom-call(f32[8]{0:T(128)S(1)} %convert_rsqrt_fusion.factors, bf16[256,256]{1,0:T(8,128)(2,1)S(1)} %bitcast.30, bf16[256,256]{1,0:T(8,128)(2,1)S(1)} %collective-permute-done.21.refs_1_, bf16[256,256]{1,0:T(8,128)(2,1)S(1)} %collective-permute-done.22.refs_2_, ...), custom_call_target="tpu_custom_call" | custom-call | flops 4294967296 | bytes 16777216 | tf_op jit(solution)/shard_map/correlate/pallas_call | solution.py:370
  112.3 0.0 collective-permute-done.17.refs_3_
  112.3 0.0 collective-permute-done.16.refs_2_
  112.3 0.0 collective-permute-done.15.refs_1_
  112.3 0.1 pad_maximum_fusion.3
  112.4 0.1 collective-permute-start.25
  112.5 1.9 %collective-permute-done.25.refs_4_ = bf16[4,256,256]{2,1,0:T(8,128)(2,1)S(1)} collective-permute-done((bf16[4,256,256]{2,1,0:T(8,128)(2,1)S(1)}, bf16[4,256,256]{2,1,0:T(8,128)(2,1)S(1)}, u32[]{:S(2)}, u32[]{:S(2)}) %collective-permute-start.25) | collective-permute-done | bytes 524320 | tf_op jit(solution)/shard_map/ppermute | solution.py:22
  114.3 8.2 %correlate.3 = f32[8,1024,512]{2,1,0:T(8,128)} custom-call(f32[8]{0:T(128)S(1)} %convert_rsqrt_fusion.factors, bf16[256,256]{1,0:T(8,128)(2,1)S(1)} %get-tuple-element.37.refs_0_, bf16[256,256]{1,0:T(8,128)(2,1)S(1)} %collective-permute-done.15.refs_1_, bf16[256,256]{1,0:T(8,128)(2,1)S(1)} %collective-permute-done.16.refs_2_, ...), custom_call_target="tpu_custom_call", output_to_operand_aliasing={{}: (7, {})} | custom-call | flops 4294967296 | bytes 16777216 | tf_op jit(solution)/shard_map/correlate/pallas_call | solution.py:370
  (12 shorter events, 0.2 us)
Async XLA Ops:
  20.6 19.0 %collective-permute-start = (f32[256,256]{1,0:T(8,128)S(1)}, f32[256,256]{1,0:T(8,128)S(1)}, u32[]{:S(2)}, u32[]{:S(2)}) collective-permute-start(f32[256,256]{1,0:T(8,128)S(1)} %get-tuple-element.26), channel_id=1, source_target_pairs={{0,16},{8,24},{16,0},{24,8},{1,17},{9,25},{17,1},{25,9},{2,18},{10... | collective-permute-start | bytes 786440 | tf_op jit(solution)/shard_map/ppermute | solution.py:22
  23.6 11.9 %collective-permute-start.1 = (f32[256,256]{1,0:T(8,128)S(1)}, f32[256,256]{1,0:T(8,128)S(1)}, u32[]{:S(2)}, u32[]{:S(2)}) collective-permute-start(f32[256,256]{1,0:T(8,128)S(1)} %get-tuple-element.28), channel_id=1, source_target_pairs={{0,16},{8,24},{16,0},{24,8},{1,17},{9,25},{17,1},{25,9},{2,18},{10... | collective-permute-start | bytes 786440 | tf_op jit(solution)/shard_map/ppermute | solution.py:22
  23.7 14.0 %collective-permute-start.4 = (f32[256,256]{1,0:T(8,128)S(1)}, f32[256,256]{1,0:T(8,128)S(1)}, u32[]{:S(2)}, u32[]{:S(2)}) collective-permute-start(f32[256,256]{1,0:T(8,128)S(1)} %get-tuple-element.32), channel_id=1, source_target_pairs={{0,8},{8,0},{16,24},{24,16},{1,9},{9,1},{17,25},{25,17},{2,10},{10... | collective-permute-start | bytes 786440 | tf_op jit(solution)/shard_map/ppermute | solution.py:22
  25.6 66.2 %copy-start = (s32[8]{0:T(128)S(1)}, s32[8]{0:T(128)}, u32[]{:S(2)}) copy-start(s32[8]{0:T(128)} %offsets.1) | copy-start | bytes 100
  35.6 9.2 %collective-permute-start.2 = (f32[256,256]{1,0:T(8,128)S(1)}, f32[256,256]{1,0:T(8,128)S(1)}, u32[]{:S(2)}, u32[]{:S(2)}) collective-permute-start(f32[256,256]{1,0:T(8,128)S(1)} %add.55), channel_id=1, source_target_pairs={{0,8},{8,0},{16,24},{24,16},{1,9},{9,1},{17,25},{25,17},{2,10},{10... | collective-permute-start | bytes 786440 | tf_op jit(solution)/shard_map/ppermute | solution.py:22
  37.3 11.4 %collective-permute-start.3 = (f32[256,256]{1,0:T(8,128)S(1)}, f32[256,256]{1,0:T(8,128)S(1)}, u32[]{:S(2)}, u32[]{:S(2)}) collective-permute-start(f32[256,256]{1,0:T(8,128)S(1)} %get-tuple-element.30), channel_id=1, source_target_pairs={{0,8},{8,0},{16,24},{24,16},{1,9},{9,1},{17,25},{25,17},{2,10},{10... | collective-permute-start | bytes 786440 | tf_op jit(solution)/shard_map/ppermute | solution.py:22
  37.7 11.0 %collective-permute-start.5 = (f32[256,256]{1,0:T(8,128)S(1)}, f32[256,256]{1,0:T(8,128)S(1)}, u32[]{:S(2)}, u32[]{:S(2)}) collective-permute-start(f32[256,256]{1,0:T(8,128)S(1)} %add.58), channel_id=1, source_target_pairs={{0,16},{8,24},{16,0},{24,8},{1,17},{9,25},{17,1},{25,9},{2,18},{10... | collective-permute-start | bytes 786440 | tf_op jit(solution)/shard_map/ppermute | solution.py:22
  48.8 1.2 collective-permute-start.6
  50.0 3.6 %collective-permute-start.7 = (f32[256]{0:T(256)S(1)}, f32[256]{0:T(256)S(1)}, u32[]{:S(2)}, u32[]{:S(2)}) collective-permute-start(f32[256]{0:T(256)S(1)} %add.61), channel_id=1, source_target_pairs={{0,2},{1,3},{2,0},{3,1},{4,6},{5,7},{6,4},{7,5},{8,10},{9,11},{10,... | collective-permute-start | bytes 3080 | tf_op jit(solution)/shard_map/ppermute | solution.py:22
  53.6 4.5 %collective-permute-start.8 = (f32[256]{0:T(256)S(1)}, f32[256]{0:T(256)S(1)}, u32[]{:S(2)}, u32[]{:S(2)}) collective-permute-start(f32[256]{0:T(256)S(1)} %add.62), channel_id=1, source_target_pairs={{0,4},{1,5},{2,6},{3,7},{4,0},{5,1},{6,2},{7,3},{8,12},{9,13},{10,... | collective-permute-start | bytes 3080 | tf_op jit(solution)/shard_map/ppermute | solution.py:22
  58.2 7.8 %collective-permute-start.20 = (bf16[256,256]{1,0:T(8,128)(2,1)S(1)}, bf16[256,256]{1,0:T(8,128)(2,1)S(1)}, u32[]{:S(2)}, u32[]{:S(2)}) collective-permute-start(bf16[256,256]{1,0:T(8,128)(2,1)S(1)} %get-tuple-element.51), channel_id=1, source_target_pairs={{0,6},{1,7},{2,4},{3,5},{4,2},{5,3},{6,0},{7,1},{8,14},{9,15},{10,... | collective-permute-start | bytes 393224 | tf_op jit(solution)/shard_map/ppermute | solution.py:22
  61.8 9.1 %collective-permute-start.19 = (bf16[256,256]{1,0:T(8,128)(2,1)S(1)}, bf16[256,256]{1,0:T(8,128)(2,1)S(1)}, u32[]{:S(2)}, u32[]{:S(2)}) collective-permute-start(bf16[256,256]{1,0:T(8,128)(2,1)S(1)} %get-tuple-element.51), channel_id=1, source_target_pairs={{0,4},{1,5},{2,6},{3,7},{4,0},{5,1},{6,2},{7,3},{8,12},{9,13},{10,... | collective-permute-start | bytes 393224 | tf_op jit(solution)/shard_map/ppermute | solution.py:22
  61.8 9.1 %collective-permute-start.18 = (bf16[256,256]{1,0:T(8,128)(2,1)S(1)}, bf16[256,256]{1,0:T(8,128)(2,1)S(1)}, u32[]{:S(2)}, u32[]{:S(2)}) collective-permute-start(bf16[256,256]{1,0:T(8,128)(2,1)S(1)} %get-tuple-element.51), channel_id=1, source_target_pairs={{0,2},{1,3},{2,0},{3,1},{4,6},{5,7},{6,4},{7,5},{8,10},{9,11},{10,... | collective-permute-start | bytes 393224 | tf_op jit(solution)/shard_map/ppermute | solution.py:22
  71.1 6.7 %collective-permute-start.23 = (bf16[256,256]{1,0:T(8,128)(2,1)S(1)}, bf16[256,256]{1,0:T(8,128)(2,1)S(1)}, u32[]{:S(2)}, u32[]{:S(2)}) collective-permute-start(bf16[256,256]{1,0:T(8,128)(2,1)S(1)} %get-tuple-element.43), channel_id=1, source_target_pairs={{0,24},{8,16},{16,8},{24,0},{1,25},{9,17},{17,9},{25,1},{2,26},{10... | collective-permute-start | bytes 393224 | tf_op jit(solution)/shard_map/ppermute | solution.py:22
  73.6 12.3 %collective-permute-start.22 = (bf16[256,256]{1,0:T(8,128)(2,1)S(1)}, bf16[256,256]{1,0:T(8,128)(2,1)S(1)}, u32[]{:S(2)}, u32[]{:S(2)}) collective-permute-start(bf16[256,256]{1,0:T(8,128)(2,1)S(1)} %get-tuple-element.44), channel_id=1, source_target_pairs={{0,16},{8,24},{16,0},{24,8},{1,17},{9,25},{17,1},{25,9},{2,18},{10... | collective-permute-start | bytes 393224 | tf_op jit(solution)/shard_map/ppermute | solution.py:22
  74.1 11.8 %collective-permute-start.21 = (bf16[256,256]{1,0:T(8,128)(2,1)S(1)}, bf16[256,256]{1,0:T(8,128)(2,1)S(1)}, u32[]{:S(2)}, u32[]{:S(2)}) collective-permute-start(bf16[256,256]{1,0:T(8,128)(2,1)S(1)} %get-tuple-element.45), channel_id=1, source_target_pairs={{0,8},{8,0},{16,24},{24,16},{1,9},{9,1},{17,25},{25,17},{2,10},{10... | collective-permute-start | bytes 393224 | tf_op jit(solution)/shard_map/ppermute | solution.py:22
  74.7 14.8 %collective-permute-start.14 = (bf16[512,256]{1,0:T(8,128)(2,1)S(1)}, bf16[512,256]{1,0:T(8,128)(2,1)S(1)}, u32[]{:S(2)}, u32[]{:S(2)}) collective-permute-start(bf16[512,256]{1,0:T(8,128)(2,1)S(1)} %pad_maximum_fusion.4.refs_0_), channel_id=1, source_target_pairs={{0,24},{8,16},{16,8},{24,0},{1,25},{9,17},{17,9},{25,1},{2,26},{10... | collective-permute-start | bytes 786440 | tf_op jit(solution)/shard_map/ppermute | solution.py:22
  77.2 13.5 %collective-permute-start.13 = (bf16[512,256]{1,0:T(8,128)(2,1)S(1)}, bf16[512,256]{1,0:T(8,128)(2,1)S(1)}, u32[]{:S(2)}, u32[]{:S(2)}) collective-permute-start(bf16[512,256]{1,0:T(8,128)(2,1)S(1)} %pad_maximum_fusion.4.refs_0_), channel_id=1, source_target_pairs={{0,16},{8,24},{16,0},{24,8},{1,17},{9,25},{17,1},{25,9},{2,18},{10... | collective-permute-start | bytes 786440 | tf_op jit(solution)/shard_map/ppermute | solution.py:22
  85.9 18.1 %collective-permute-start.24 = (bf16[4,256,256]{2,1,0:T(8,128)(2,1)S(1)}, bf16[4,256,256]{2,1,0:T(8,128)(2,1)S(1)}, u32[]{:S(2)}, u32[]{:S(2)}) collective-permute-start(bf16[4,256,256]{2,1,0:T(8,128)(2,1)S(1)} %pad_maximum_fusion.2), channel_id=1, source_target_pairs={{0,1},{1,0},{2,3},{3,2},{4,5},{5,4},{6,7},{7,6},{8,9},{9,8},{10,11... | collective-permute-start | bytes 1572872 | tf_op jit(solution)/shard_map/ppermute | solution.py:22
  86.0 8.7 %collective-permute-start.12 = (bf16[512,256]{1,0:T(8,128)(2,1)S(1)}, bf16[512,256]{1,0:T(8,128)(2,1)S(1)}, u32[]{:S(2)}, u32[]{:S(2)}) collective-permute-start(bf16[512,256]{1,0:T(8,128)(2,1)S(1)} %pad_maximum_fusion.4.refs_0_), channel_id=1, source_target_pairs={{0,8},{8,0},{16,24},{24,16},{1,9},{9,1},{17,25},{25,17},{2,10},{10... | collective-permute-start | bytes 786440 | tf_op jit(solution)/shard_map/ppermute | solution.py:22
  87.4 9.8 %collective-permute-start.11 = (bf16[256,256]{1,0:T(8,128)(2,1)S(1)}, bf16[256,256]{1,0:T(8,128)(2,1)S(1)}, u32[]{:S(2)}, u32[]{:S(2)}) collective-permute-start(bf16[256,256]{1,0:T(8,128)(2,1)S(1)} %get-tuple-element.33), channel_id=1, source_target_pairs={{0,6},{1,7},{2,4},{3,5},{4,2},{5,3},{6,0},{7,1},{8,14},{9,15},{10,... | collective-permute-start | bytes 393224 | tf_op jit(solution)/shard_map/ppermute | solution.py:22
  89.4 11.0 %collective-permute-start.10 = (bf16[256,256]{1,0:T(8,128)(2,1)S(1)}, bf16[256,256]{1,0:T(8,128)(2,1)S(1)}, u32[]{:S(2)}, u32[]{:S(2)}) collective-permute-start(bf16[256,256]{1,0:T(8,128)(2,1)S(1)} %get-tuple-element.33), channel_id=1, source_target_pairs={{0,4},{1,5},{2,6},{3,7},{4,0},{5,1},{6,2},{7,3},{8,12},{9,13},{10,... | collective-permute-start | bytes 393224 | tf_op jit(solution)/shard_map/ppermute | solution.py:22
  90.7 9.7 %collective-permute-start.9 = (bf16[256,256]{1,0:T(8,128)(2,1)S(1)}, bf16[256,256]{1,0:T(8,128)(2,1)S(1)}, u32[]{:S(2)}, u32[]{:S(2)}) collective-permute-start(bf16[256,256]{1,0:T(8,128)(2,1)S(1)} %get-tuple-element.33), channel_id=1, source_target_pairs={{0,2},{1,3},{2,0},{3,1},{4,6},{5,7},{6,4},{7,5},{8,10},{9,11},{10,... | collective-permute-start | bytes 393224 | tf_op jit(solution)/shard_map/ppermute | solution.py:22
  100.5 11.8 %collective-permute-start.17 = (bf16[256,256]{1,0:T(8,128)(2,1)S(1)}, bf16[256,256]{1,0:T(8,128)(2,1)S(1)}, u32[]{:S(2)}, u32[]{:S(2)}) collective-permute-start(bf16[256,256]{1,0:T(8,128)(2,1)S(1)} %get-tuple-element.47), channel_id=1, source_target_pairs={{0,24},{8,16},{16,8},{24,0},{1,25},{9,17},{17,9},{25,1},{2,26},{10... | collective-permute-start | bytes 393224 | tf_op jit(solution)/shard_map/ppermute | solution.py:22
  102.0 10.2 %collective-permute-start.16 = (bf16[256,256]{1,0:T(8,128)(2,1)S(1)}, bf16[256,256]{1,0:T(8,128)(2,1)S(1)}, u32[]{:S(2)}, u32[]{:S(2)}) collective-permute-start(bf16[256,256]{1,0:T(8,128)(2,1)S(1)} %get-tuple-element.48), channel_id=1, source_target_pairs={{0,16},{8,24},{16,0},{24,8},{1,17},{9,25},{17,1},{25,9},{2,18},{10... | collective-permute-start | bytes 393224 | tf_op jit(solution)/shard_map/ppermute | solution.py:22
  102.7 9.5 %collective-permute-start.15 = (bf16[256,256]{1,0:T(8,128)(2,1)S(1)}, bf16[256,256]{1,0:T(8,128)(2,1)S(1)}, u32[]{:S(2)}, u32[]{:S(2)}) collective-permute-start(bf16[256,256]{1,0:T(8,128)(2,1)S(1)} %get-tuple-element.49), channel_id=1, source_target_pairs={{0,8},{8,0},{16,24},{24,16},{1,9},{9,1},{17,25},{25,17},{2,10},{10... | collective-permute-start | bytes 393224 | tf_op jit(solution)/shard_map/ppermute | solution.py:22
  112.4 2.0 %collective-permute-start.25 = (bf16[4,256,256]{2,1,0:T(8,128)(2,1)S(1)}, bf16[4,256,256]{2,1,0:T(8,128)(2,1)S(1)}, u32[]{:S(2)}, u32[]{:S(2)}) collective-permute-start(bf16[4,256,256]{2,1,0:T(8,128)(2,1)S(1)} %pad_maximum_fusion.3), channel_id=1, source_target_pairs={{0,1},{1,0},{2,3},{3,2},{4,5},{5,4},{6,7},{7,6},{8,9},{9,8},{10,11... | collective-permute-start | bytes 1572872 | tf_op jit(solution)/shard_map/ppermute | solution.py:22
where the time goes:
time: 123 us
  Pallas kernels  46 us (37%)
  waiting for transfers between devices  43.4 us (35%)
  starting transfers between devices  32.3 us (26%)
    ppermute x26, waiting for transfers between devices, swap(): return lax.ppermute(block, axis, [(i, i ^ offset) for i in range(size)])  43.4 us
    ppermute x26, starting transfers between devices, swap(): return lax.ppermute(block, axis, [(i, i ^ offset) for i in range(size)])  32.3 us
    pallas_call x1, Pallas kernels, reorder_project(): pl.pallas_call(functools.partial(reorder_project_kernel, chunk=chunk, ord...  20.5 us
    pallas_call x2, Pallas kernels, correlate(): pl.pallas_call(functools.partial(correlate_kernel, parts=parts, owners=ow...  16.4 us
    pallas_call x1, Pallas kernels, project(): pl.pallas_call(functools.partial(project_kernel, chunk=chunk, order=order...  6.57 us
    pallas_call x1, Pallas kernels, shifted_copies(): pl.pallas_call(functools.partial(shift_kernel, parts=parts), out_shape=ja...  2.48 us
  transfers between devices with their start and end apart: 26, of which 14 were waited for; matrix products, arithmetic and copies ran while one was open for 0% of the time, Pallas kernels for 14%

commit v1 on v0

--- a/solution.py
+++ b/solution.py
@@ -13,6 +13,7 @@
 ROWS = 8
 GROUP = 16
 MARGIN = 3 << 20
+STEPS = 2
 
 epsilon = 1e-06
 
@@ -46,7 +47,7 @@
             ] = jnp.concatenate(tiles, axis=0).astype(jnp.bfloat16)
         return carry
 
-    lax.fori_loop(0, groups, move, 0, unroll=8)
+    lax.fori_loop(0, groups, move, 0, unroll=2)
 
 
 def arrangement(lists):
@@ -81,14 +82,14 @@
             outs[h * count + i][...] = total[i * size : (i + 1) * size, h * half : (h + 1) * half].T
 
 
-def reorder_project_kernel(slot, panel, velocities, *refs, chunk, order, runs):
+def reorder_project_kernel(slot, panel, velocities, *refs, chunk, block, order, runs):
     count = runs[0][1]
     outs, ordered_out = refs[: 2 * count], refs[2 * count]
     tripled, slots, staged, source, rows, total, slot_sem, in_sems, row_sems, out_sem = refs[2 * count + 1 :]
     depth, width = panel.shape
     blocks = width // LANES
     size = outs[0].shape[1]
-    chunks = depth // chunk
+    chunks, steps = depth // chunk, depth // block
     starts = row_starts(order, size)
 
     def panel_copy(c):
@@ -96,7 +97,7 @@
         return pltpu.make_async_copy(panel.at[part, :], staged.at[part, :], in_sems.at[c])
 
     def row_copy(i, c):
-        part = pl.ds(pl.multiple_of(c * chunk, chunk), chunk)
+        part = pl.ds(pl.multiple_of(c * block, block), block)
         return pltpu.make_async_copy(
             velocities.at[pl.ds(starts[i], size), part],
             rows.at[pl.ds(i * size, size), part],
@@ -104,16 +105,13 @@
         )
 
     def ordered_copy(c):
-        part = pl.ds(pl.multiple_of(c * chunk, chunk), chunk)
+        part = pl.ds(pl.multiple_of(c * block, block), block)
         return pltpu.make_async_copy(staged.at[part, :], ordered_out.at[part, :], out_sem)
 
     first_copy = pltpu.make_async_copy(slot, tripled, slot_sem)
     first_copy.start()
     for c in range(chunks):
         panel_copy(c).start()
-    for c in range(chunks):
-        for i in range(len(order)):
-            row_copy(i, c).start()
     first_copy.wait()
     tripled[...] = tripled[...] * 3
     slot_copy = pltpu.make_async_copy(tripled, slots, slot_sem)
@@ -131,20 +129,24 @@
             return carry
 
         lax.fori_loop(0, chunk // LANES, widen, 0)
+        later = c - (chunks - steps)
+        if later >= 0:
+            for i in range(len(order)):
+                row_copy(i, later).start()
     slot_copy.wait()
 
     def body(c, carry):
-        reorder_chunk(slots, source, staged, chunk, c)
+        reorder_chunk(slots, source, staged, block, c)
         ordered_copy(c).start()
         for i in range(len(order)):
             row_copy(i, c).wait()
-        part = pl.ds(pl.multiple_of(c * chunk, chunk), chunk)
+        part = pl.ds(pl.multiple_of(c * block, block), block)
         add_products(total, rows, part, staged, runs, size)
         return carry
 
-    lax.fori_loop(0, chunks, body, 0)
+    lax.fori_loop(0, steps, body, 0)
     write_turned(total, outs)
-    for c in range(chunks):
+    for c in range(steps):
         ordered_copy(c).wait()
 
 
@@ -152,11 +154,11 @@
     depth, width = panel.shape
     order, runs = arrangement(lists)
     count = runs[0][1]
-    chunk = depth // 10
+    chunk, block = depth // 5, depth // STEPS
     anywhere = pl.BlockSpec(memory_space=pl.ANY)
     part = jax.ShapeDtypeStruct((width // 2, size), jnp.float32)
     *parts, ordered = pl.pallas_call(
-        functools.partial(reorder_project_kernel, chunk=chunk, order=order, runs=runs),
+        functools.partial(reorder_project_kernel, chunk=chunk, block=block, order=order, runs=runs),
         out_shape=[part] * (2 * count) + [jax.ShapeDtypeStruct((depth, width), jnp.bfloat16)],
         grid=(1,),
         in_specs=[pl.BlockSpec(memory_space=pltpu.HBM)] * 3,
@@ -170,7 +172,7 @@
             pltpu.VMEM((count * size, width), jnp.float32),
             pltpu.SemaphoreType.DMA,
             pltpu.SemaphoreType.DMA((depth // chunk,)),
-            pltpu.SemaphoreType.DMA((depth // chunk, len(order))),
+            pltpu.SemaphoreType.DMA((depth // block, len(order))),
             pltpu.SemaphoreType.DMA,
         ],
         cost_estimate=pl.CostEstimate(

time: 123 us -> 117 us (0.951)
  Pallas kernels: 46 us -> 40 us
    pallas_call x1, Pallas kernels: 20.5 us -> 14.6 us  [reorder_project(): pl.pallas_call(functools.partial(reorder_project_kernel, chunk=chunk, blo...]
  transfers between devices with their start and end apart: 26 -> 26, of which waited for: 14 -> 14; matrix products, arithmetic and copies ran while one was open for 0% -> 0% of each run, Pallas kernels for 14% -> 15%
where the time goes in v1:
time: 117 us
  waiting for transfers between devices  43.3 us (37%)
  Pallas kernels  40 us (34%)
  starting transfers between devices  32.3 us (28%)
    ppermute x26, waiting for transfers between devices, swap(): return lax.ppermute(block, axis, [(i, i ^ offset) for i in range(size)])  43.3 us
    ppermute x26, starting transfers between devices, swap(): return lax.ppermute(block, axis, [(i, i ^ offset) for i in range(size)])  32.3 us
    pallas_call x2, Pallas kernels, correlate(): pl.pallas_call(functools.partial(correlate_kernel, parts=parts, owners=ow...  16.4 us
    pallas_call x1, Pallas kernels, reorder_project(): pl.pallas_call(functools.partial(reorder_project_kernel, chunk=chunk, blo...  14.6 us
    pallas_call x1, Pallas kernels, project(): pl.pallas_call(functools.partial(project_kernel, chunk=chunk, order=order...  6.57 us
    pallas_call x1, Pallas kernels, shifted_copies(): pl.pallas_call(functools.partial(shift_kernel, parts=parts), out_shape=ja...  2.48 us
  transfers between devices with their start and end apart: 26, of which 14 were waited for; matrix products, arithmetic and copies ran while one was open for 0% of the time, Pallas kernels for 15%

profile of v1, /device:TPU:0, one launch (start us, length us, event | category | flops | bytes accessed | tf_op | source)
XLA Modules:
  0.0 116.6 jit_solution(15077659815635914318)
XLA Ops:
  0.0 14.6 %reorder_project.1 = (f32[256,256]{1,0:T(8,128)S(1)}, f32[256,256]{1,0:T(8,128)S(1)}, f32[256,256]{1,0:T(8,128)S(1)}, f32[256,256]{1,0:T(8,128)S(1)}, bf16[7680,512]{1,0:T(8,128)(2,1)S(1)}) custom-call(s32[2560]{0:T(1024)} %slot.1, bf16[7680,512]{1,0:T(8,128)(2,1)} %panel.1, bf16[1024,7680]{1,0:T(8,128)(2,1)} %velocities.3), custom_call_target="tpu_custom_call" | custom-call | flops 4026531840 | bytes 23592960 | tf_op jit(solution)/shard_map/reorder_project/pallas_call | solution.py:160
  14.6 3.0 %collective-permute-start = (f32[256,256]{1,0:T(8,128)S(1)}, f32[256,256]{1,0:T(8,128)S(1)}, u32[]{:S(2)}, u32[]{:S(2)}) collective-permute-start(f32[256,256]{1,0:T(8,128)S(1)} %get-tuple-element.26), channel_id=1, source_target_pairs={{0,16},{8,24},{16,0},{24,8},{1,17},{9,25},{17,1},{25,9},{2,18},{10... | collective-permute-start | bytes 786440 | tf_op jit(solution)/shard_map/ppermute | solution.py:23
  17.6 0.1 collective-permute-start.1
  17.7 1.9 %collective-permute-start.4 = (f32[256,256]{1,0:T(8,128)S(1)}, f32[256,256]{1,0:T(8,128)S(1)}, u32[]{:S(2)}, u32[]{:S(2)}) collective-permute-start(f32[256,256]{1,0:T(8,128)S(1)} %get-tuple-element.32), channel_id=1, source_target_pairs={{0,8},{8,0},{16,24},{24,16},{1,9},{9,1},{17,25},{25,17},{2,10},{10... | collective-permute-start | bytes 786440 | tf_op jit(solution)/shard_map/ppermute | solution.py:23
  19.6 6.6 %project.1 = (f32[256,256]{1,0:T(8,128)S(1)}, f32[256,256]{1,0:T(8,128)S(1)}, f32[256,256]{1,0:T(8,128)S(1)}, f32[256,256]{1,0:T(8,128)S(1)}) custom-call(bf16[7680,512]{1,0:T(8,128)(2,1)S(1)} %get-tuple-element.24.panel, bf16[1024,7680]{1,0:T(8,128)(2,1)} %velocities.3), custom_call_target="tpu_custom_call" | custom-call | flops 4026531840 | bytes 19660800 | tf_op jit(solution)/shard_map/project/pallas_call | solution.py:232
  26.2 3.3 %collective-permute-done.1 = f32[256,256]{1,0:T(8,128)S(1)} collective-permute-done((f32[256,256]{1,0:T(8,128)S(1)}, f32[256,256]{1,0:T(8,128)S(1)}, u32[]{:S(2)}, u32[]{:S(2)}) %collective-permute-start.1) | collective-permute-done | bytes 262176 | tf_op jit(solution)/shard_map/ppermute | solution.py:23
  29.6 1.8 %collective-permute-start.2 = (f32[256,256]{1,0:T(8,128)S(1)}, f32[256,256]{1,0:T(8,128)S(1)}, u32[]{:S(2)}, u32[]{:S(2)}) collective-permute-start(f32[256,256]{1,0:T(8,128)S(1)} %add.55), channel_id=1, source_target_pairs={{0,8},{8,0},{16,24},{24,16},{1,9},{9,1},{17,25},{25,17},{2,10},{10... | collective-permute-start | bytes 786440 | tf_op jit(solution)/shard_map/ppermute | solution.py:23
  31.4 0.3 collective-permute-start.3
  31.7 0.0 collective-permute-done.4
  31.7 1.8 %collective-permute-start.5 = (f32[256,256]{1,0:T(8,128)S(1)}, f32[256,256]{1,0:T(8,128)S(1)}, u32[]{:S(2)}, u32[]{:S(2)}) collective-permute-start(f32[256,256]{1,0:T(8,128)S(1)} %add.58), channel_id=1, source_target_pairs={{0,16},{8,24},{16,0},{24,8},{1,17},{9,25},{17,1},{25,9},{2,18},{10... | collective-permute-start | bytes 786440 | tf_op jit(solution)/shard_map/ppermute | solution.py:23
  33.5 0.0 collective-permute-done
  33.5 5.3 %collective-permute-done.2 = f32[256,256]{1,0:T(8,128)S(1)} collective-permute-done((f32[256,256]{1,0:T(8,128)S(1)}, f32[256,256]{1,0:T(8,128)S(1)}, u32[]{:S(2)}, u32[]{:S(2)}) %collective-permute-start.2) | collective-permute-done | bytes 262176 | tf_op jit(solution)/shard_map/ppermute | solution.py:23
  38.8 0.1 multiply_reduce_fusion
  38.9 3.8 %collective-permute-done.3 = f32[256,256]{1,0:T(8,128)S(1)} collective-permute-done((f32[256,256]{1,0:T(8,128)S(1)}, f32[256,256]{1,0:T(8,128)S(1)}, u32[]{:S(2)}, u32[]{:S(2)}) %collective-permute-start.3) | collective-permute-done | bytes 262176 | tf_op jit(solution)/shard_map/ppermute | solution.py:23
  42.7 0.0 collective-permute-done.5
  42.7 0.1 multiply_reduce_fusion.1
  42.8 0.1 collective-permute-start.6
  42.9 1.1 collective-permute-done.6
  44.0 1.5 %collective-permute-start.7 = (f32[256]{0:T(256)S(1)}, f32[256]{0:T(256)S(1)}, u32[]{:S(2)}, u32[]{:S(2)}) collective-permute-start(f32[256]{0:T(256)S(1)} %add.61), channel_id=1, source_target_pairs={{0,2},{1,3},{2,0},{3,1},{4,6},{5,7},{6,4},{7,5},{8,10},{9,11},{10,... | collective-permute-start | bytes 3080 | tf_op jit(solution)/shard_map/ppermute | solution.py:23
  45.6 2.0 %collective-permute-done.7 = f32[256]{0:T(256)S(1)} collective-permute-done((f32[256]{0:T(256)S(1)}, f32[256]{0:T(256)S(1)}, u32[]{:S(2)}, u32[]{:S(2)}) %collective-permute-start.7) | collective-permute-done | bytes 1056 | tf_op jit(solution)/shard_map/ppermute | solution.py:23
  47.6 2.6 %collective-permute-start.8 = (f32[256]{0:T(256)S(1)}, f32[256]{0:T(256)S(1)}, u32[]{:S(2)}, u32[]{:S(2)}) collective-permute-start(f32[256]{0:T(256)S(1)} %add.62), channel_id=1, source_target_pairs={{0,4},{1,5},{2,6},{3,7},{4,0},{5,1},{6,2},{7,3},{8,12},{9,13},{10,... | collective-permute-start | bytes 3080 | tf_op jit(solution)/shard_map/ppermute | solution.py:23
  50.2 1.9 %collective-permute-done.8 = f32[256]{0:T(256)S(1)} collective-permute-done((f32[256]{0:T(256)S(1)}, f32[256]{0:T(256)S(1)}, u32[]{:S(2)}, u32[]{:S(2)}) %collective-permute-start.8) | collective-permute-done | bytes 1056 | tf_op jit(solution)/shard_map/ppermute | solution.py:23
  52.1 0.1 multiply_convert_fusion
  52.2 3.6 %collective-permute-start.20 = (bf16[256,256]{1,0:T(8,128)(2,1)S(1)}, bf16[256,256]{1,0:T(8,128)(2,1)S(1)}, u32[]{:S(2)}, u32[]{:S(2)}) collective-permute-start(bf16[256,256]{1,0:T(8,128)(2,1)S(1)} %get-tuple-element.51), channel_id=1, source_target_pairs={{0,6},{1,7},{2,4},{3,5},{4,2},{5,3},{6,0},{7,1},{8,14},{9,15},{10,... | collective-permute-start | bytes 393224 | tf_op jit(solution)/shard_map/ppermute | solution.py:23
  55.9 0.0 collective-permute-start.19
  55.9 0.8 collective-permute-start.18
  56.7 3.3 %collective-permute-done.20 = bf16[256,256]{1,0:T(8,128)(2,1)S(1)} collective-permute-done((bf16[256,256]{1,0:T(8,128)(2,1)S(1)}, bf16[256,256]{1,0:T(8,128)(2,1)S(1)}, u32[]{:S(2)}, u32[]{:S(2)}) %collective-permute-start.20) | collective-permute-done | bytes 131104 | tf_op jit(solution)/shard_map/ppermute | solution.py:23
  60.0 5.0 %collective-permute-done.19 = bf16[256,256]{1,0:T(8,128)(2,1)S(1)} collective-permute-done((bf16[256,256]{1,0:T(8,128)(2,1)S(1)}, bf16[256,256]{1,0:T(8,128)(2,1)S(1)}, u32[]{:S(2)}, u32[]{:S(2)}) %collective-permute-start.19) | collective-permute-done | bytes 131104 | tf_op jit(solution)/shard_map/ppermute | solution.py:23
  65.0 0.0 collective-permute-done.18
  65.0 0.1 pad_maximum_fusion.1
  65.1 2.5 %collective-permute-start.23 = (bf16[256,256]{1,0:T(8,128)(2,1)S(1)}, bf16[256,256]{1,0:T(8,128)(2,1)S(1)}, u32[]{:S(2)}, u32[]{:S(2)}) collective-permute-start(bf16[256,256]{1,0:T(8,128)(2,1)S(1)} %get-tuple-element.43), channel_id=1, source_target_pairs={{0,24},{8,16},{16,8},{24,0},{1,25},{9,17},{17,9},{25,1},{2,26},{10... | collective-permute-start | bytes 393224 | tf_op jit(solution)/shard_map/ppermute | solution.py:23
  67.6 0.5 collective-permute-start.22
  68.1 0.6 collective-permute-start.21
  68.7 2.5 %collective-permute-start.14 = (bf16[512,256]{1,0:T(8,128)(2,1)S(1)}, bf16[512,256]{1,0:T(8,128)(2,1)S(1)}, u32[]{:S(2)}, u32[]{:S(2)}) collective-permute-start(bf16[512,256]{1,0:T(8,128)(2,1)S(1)} %pad_maximum_fusion.4.refs_0_), channel_id=1, source_target_pairs={{0,24},{8,16},{16,8},{24,0},{1,25},{9,17},{17,9},{25,1},{2,26},{10... | collective-permute-start | bytes 786440 | tf_op jit(solution)/shard_map/ppermute | solution.py:23
  71.2 0.5 collective-permute-start.13
  71.6 0.1 collective-permute-done.23.refs_3_
  71.8 8.1 %collective-permute-done.22.refs_2_ = bf16[256,256]{1,0:T(8,128)(2,1)S(1)} collective-permute-done((bf16[256,256]{1,0:T(8,128)(2,1)S(1)}, bf16[256,256]{1,0:T(8,128)(2,1)S(1)}, u32[]{:S(2)}, u32[]{:S(2)}) %collective-permute-start.22) | collective-permute-done | bytes 131104 | tf_op jit(solution)/shard_map/ppermute | solution.py:23
  79.9 0.0 collective-permute-done.21.refs_1_
  79.9 0.1 pad_maximum_fusion.2
  80.0 0.1 collective-permute-start.24
  80.0 1.4 %collective-permute-start.12 = (bf16[512,256]{1,0:T(8,128)(2,1)S(1)}, bf16[512,256]{1,0:T(8,128)(2,1)S(1)}, u32[]{:S(2)}, u32[]{:S(2)}) collective-permute-start(bf16[512,256]{1,0:T(8,128)(2,1)S(1)} %pad_maximum_fusion.4.refs_0_), channel_id=1, source_target_pairs={{0,8},{8,0},{16,24},{24,16},{1,9},{9,1},{17,25},{25,17},{2,10},{10... | collective-permute-start | bytes 786440 | tf_op jit(solution)/shard_map/ppermute | solution.py:23
  81.4 2.0 %collective-permute-start.11 = (bf16[256,256]{1,0:T(8,128)(2,1)S(1)}, bf16[256,256]{1,0:T(8,128)(2,1)S(1)}, u32[]{:S(2)}, u32[]{:S(2)}) collective-permute-start(bf16[256,256]{1,0:T(8,128)(2,1)S(1)} %get-tuple-element.33), channel_id=1, source_target_pairs={{0,6},{1,7},{2,4},{3,5},{4,2},{5,3},{6,0},{7,1},{8,14},{9,15},{10,... | collective-permute-start | bytes 393224 | tf_op jit(solution)/shard_map/ppermute | solution.py:23
  83.4 0.0 collective-permute-done.14.refs_3_
  83.4 0.0 collective-permute-start.10
  83.4 1.2 %collective-permute-done.13.refs_2_ = bf16[512,256]{1,0:T(8,128)(2,1)S(1)} collective-permute-done((bf16[512,256]{1,0:T(8,128)(2,1)S(1)}, bf16[512,256]{1,0:T(8,128)(2,1)S(1)}, u32[]{:S(2)}, u32[]{:S(2)}) %collective-permute-start.13) | collective-permute-done | bytes 262176 | tf_op jit(solution)/shard_map/ppermute | solution.py:23
  84.6 1.2 %collective-permute-start.9 = (bf16[256,256]{1,0:T(8,128)(2,1)S(1)}, bf16[256,256]{1,0:T(8,128)(2,1)S(1)}, u32[]{:S(2)}, u32[]{:S(2)}) collective-permute-start(bf16[256,256]{1,0:T(8,128)(2,1)S(1)} %get-tuple-element.33), channel_id=1, source_target_pairs={{0,2},{1,3},{2,0},{3,1},{4,6},{5,7},{6,4},{7,5},{8,10},{9,11},{10,... | collective-permute-start | bytes 393224 | tf_op jit(solution)/shard_map/ppermute | solution.py:23
  85.8 2.9 %collective-permute-done.12.refs_1_ = bf16[512,256]{1,0:T(8,128)(2,1)S(1)} collective-permute-done((bf16[512,256]{1,0:T(8,128)(2,1)S(1)}, bf16[512,256]{1,0:T(8,128)(2,1)S(1)}, u32[]{:S(2)}, u32[]{:S(2)}) %collective-permute-start.12) | collective-permute-done | bytes 262176 | tf_op jit(solution)/shard_map/ppermute | solution.py:23
  88.7 2.5 %shift.1.refs_5_ = bf16[8,1024,512]{2,1,0:T(8,128)(2,1)S(1)} custom-call(s32[8]{0:T(128)S(1)} %copy-done, bf16[512,256]{1,0:T(8,128)(2,1)S(1)} %pad_maximum_fusion.4.refs_0_, bf16[512,256]{1,0:T(8,128)(2,1)S(1)} %collective-permute-done.12.refs_1_, bf16[512,256]{1,0:T(8,128)(2,1)S(1)} %collective-permute-done.13.refs_2_, ...), custom_call_target="tpu_custom_call" | custom-call | bytes 9437184 | tf_op jit(solution)/shard_map/shift/pallas_call | solution.py:292
  91.2 0.0 collective-permute-done.11
  91.2 3.2 %collective-permute-done.10 = bf16[256,256]{1,0:T(8,128)(2,1)S(1)} collective-permute-done((bf16[256,256]{1,0:T(8,128)(2,1)S(1)}, bf16[256,256]{1,0:T(8,128)(2,1)S(1)}, u32[]{:S(2)}, u32[]{:S(2)}) %collective-permute-start.10) | collective-permute-done | bytes 131104 | tf_op jit(solution)/shard_map/ppermute | solution.py:23
  94.4 0.0 collective-permute-done.9
  94.4 0.1 pad_maximum_fusion
  94.5 1.5 %collective-permute-start.17 = (bf16[256,256]{1,0:T(8,128)(2,1)S(1)}, bf16[256,256]{1,0:T(8,128)(2,1)S(1)}, u32[]{:S(2)}, u32[]{:S(2)}) collective-permute-start(bf16[256,256]{1,0:T(8,128)(2,1)S(1)} %get-tuple-element.47), channel_id=1, source_target_pairs={{0,24},{8,16},{16,8},{24,0},{1,25},{9,17},{17,9},{25,1},{2,26},{10... | collective-permute-start | bytes 393224 | tf_op jit(solution)/shard_map/ppermute | solution.py:23
  96.0 0.7 collective-permute-start.16
  96.8 1.3 %collective-permute-start.15 = (bf16[256,256]{1,0:T(8,128)(2,1)S(1)}, bf16[256,256]{1,0:T(8,128)(2,1)S(1)}, u32[]{:S(2)}, u32[]{:S(2)}) collective-permute-start(bf16[256,256]{1,0:T(8,128)(2,1)S(1)} %get-tuple-element.49), channel_id=1, source_target_pairs={{0,8},{8,0},{16,24},{24,16},{1,9},{9,1},{17,25},{25,17},{2,10},{10... | collective-permute-start | bytes 393224 | tf_op jit(solution)/shard_map/ppermute | solution.py:23
  98.1 0.0 collective-permute-done.24.refs_4_
  98.1 8.2 %correlate.2.refs_6_ = f32[8,1024,512]{2,1,0:T(8,128)} custom-call(f32[8]{0:T(128)S(1)} %convert_rsqrt_fusion.factors, bf16[256,256]{1,0:T(8,128)(2,1)S(1)} %bitcast.30, bf16[256,256]{1,0:T(8,128)(2,1)S(1)} %collective-permute-done.21.refs_1_, bf16[256,256]{1,0:T(8,128)(2,1)S(1)} %collective-permute-done.22.refs_2_, ...), custom_call_target="tpu_custom_call" | custom-call | flops 4294967296 | bytes 16777216 | tf_op jit(solution)/shard_map/correlate/pallas_call | solution.py:372
  106.3 0.0 collective-permute-done.17.refs_3_
  106.3 0.0 collective-permute-done.16.refs_2_
  106.3 0.0 collective-permute-done.15.refs_1_
  106.3 0.1 pad_maximum_fusion.3
  106.4 0.1 collective-permute-start.25
  106.5 1.9 %collective-permute-done.25.refs_4_ = bf16[4,256,256]{2,1,0:T(8,128)(2,1)S(1)} collective-permute-done((bf16[4,256,256]{2,1,0:T(8,128)(2,1)S(1)}, bf16[4,256,256]{2,1,0:T(8,128)(2,1)S(1)}, u32[]{:S(2)}, u32[]{:S(2)}) %collective-permute-start.25) | collective-permute-done | bytes 524320 | tf_op jit(solution)/shard_map/ppermute | solution.py:23
  108.4 8.2 %correlate.3 = f32[8,1024,512]{2,1,0:T(8,128)} custom-call(f32[8]{0:T(128)S(1)} %convert_rsqrt_fusion.factors, bf16[256,256]{1,0:T(8,128)(2,1)S(1)} %get-tuple-element.37.refs_0_, bf16[256,256]{1,0:T(8,128)(2,1)S(1)} %collective-permute-done.15.refs_1_, bf16[256,256]{1,0:T(8,128)(2,1)S(1)} %collective-permute-done.16.refs_2_, ...), custom_call_target="tpu_custom_call", output_to_operand_aliasing={{}: (7, {})} | custom-call | flops 4294967296 | bytes 16777216 | tf_op jit(solution)/shard_map/correlate/pallas_call | solution.py:372
  (12 shorter events, 0.2 us)
Async XLA Ops:
  14.6 18.9 %collective-permute-start = (f32[256,256]{1,0:T(8,128)S(1)}, f32[256,256]{1,0:T(8,128)S(1)}, u32[]{:S(2)}, u32[]{:S(2)}) collective-permute-start(f32[256,256]{1,0:T(8,128)S(1)} %get-tuple-element.26), channel_id=1, source_target_pairs={{0,16},{8,24},{16,0},{24,8},{1,17},{9,25},{17,1},{25,9},{2,18},{10... | collective-permute-start | bytes 786440 | tf_op jit(solution)/shard_map/ppermute | solution.py:23
  17.6 11.9 %collective-permute-start.1 = (f32[256,256]{1,0:T(8,128)S(1)}, f32[256,256]{1,0:T(8,128)S(1)}, u32[]{:S(2)}, u32[]{:S(2)}) collective-permute-start(f32[256,256]{1,0:T(8,128)S(1)} %get-tuple-element.28), channel_id=1, source_target_pairs={{0,16},{8,24},{16,0},{24,8},{1,17},{9,25},{17,1},{25,9},{2,18},{10... | collective-permute-start | bytes 786440 | tf_op jit(solution)/shard_map/ppermute | solution.py:23
  17.7 14.0 %collective-permute-start.4 = (f32[256,256]{1,0:T(8,128)S(1)}, f32[256,256]{1,0:T(8,128)S(1)}, u32[]{:S(2)}, u32[]{:S(2)}) collective-permute-start(f32[256,256]{1,0:T(8,128)S(1)} %get-tuple-element.32), channel_id=1, source_target_pairs={{0,8},{8,0},{16,24},{24,16},{1,9},{9,1},{17,25},{25,17},{2,10},{10... | collective-permute-start | bytes 786440 | tf_op jit(solution)/shard_map/ppermute | solution.py:23
  19.6 66.2 %copy-start = (s32[8]{0:T(128)S(1)}, s32[8]{0:T(128)}, u32[]{:S(2)}) copy-start(s32[8]{0:T(128)} %offsets.1) | copy-start | bytes 100
  29.6 9.2 %collective-permute-start.2 = (f32[256,256]{1,0:T(8,128)S(1)}, f32[256,256]{1,0:T(8,128)S(1)}, u32[]{:S(2)}, u32[]{:S(2)}) collective-permute-start(f32[256,256]{1,0:T(8,128)S(1)} %add.55), channel_id=1, source_target_pairs={{0,8},{8,0},{16,24},{24,16},{1,9},{9,1},{17,25},{25,17},{2,10},{10... | collective-permute-start | bytes 786440 | tf_op jit(solution)/shard_map/ppermute | solution.py:23
  31.4 11.4 %collective-permute-start.3 = (f32[256,256]{1,0:T(8,128)S(1)}, f32[256,256]{1,0:T(8,128)S(1)}, u32[]{:S(2)}, u32[]{:S(2)}) collective-permute-start(f32[256,256]{1,0:T(8,128)S(1)} %get-tuple-element.30), channel_id=1, source_target_pairs={{0,8},{8,0},{16,24},{24,16},{1,9},{9,1},{17,25},{25,17},{2,10},{10... | collective-permute-start | bytes 786440 | tf_op jit(solution)/shard_map/ppermute | solution.py:23
  31.7 11.0 %collective-permute-start.5 = (f32[256,256]{1,0:T(8,128)S(1)}, f32[256,256]{1,0:T(8,128)S(1)}, u32[]{:S(2)}, u32[]{:S(2)}) collective-permute-start(f32[256,256]{1,0:T(8,128)S(1)} %add.58), channel_id=1, source_target_pairs={{0,16},{8,24},{16,0},{24,8},{1,17},{9,25},{17,1},{25,9},{2,18},{10... | collective-permute-start | bytes 786440 | tf_op jit(solution)/shard_map/ppermute | solution.py:23
  42.8 1.2 %collective-permute-start.6 = (f32[256]{0:T(256)S(1)}, f32[256]{0:T(256)S(1)}, u32[]{:S(2)}, u32[]{:S(2)}) collective-permute-start(f32[256]{0:T(256)S(1)} %add.60), channel_id=1, source_target_pairs={{0,1},{1,0},{2,3},{3,2},{4,5},{5,4},{6,7},{7,6},{8,9},{9,8},{10,11... | collective-permute-start | bytes 3080 | tf_op jit(solution)/shard_map/ppermute | solution.py:23
  44.0 3.6 %collective-permute-start.7 = (f32[256]{0:T(256)S(1)}, f32[256]{0:T(256)S(1)}, u32[]{:S(2)}, u32[]{:S(2)}) collective-permute-start(f32[256]{0:T(256)S(1)} %add.61), channel_id=1, source_target_pairs={{0,2},{1,3},{2,0},{3,1},{4,6},{5,7},{6,4},{7,5},{8,10},{9,11},{10,... | collective-permute-start | bytes 3080 | tf_op jit(solution)/shard_map/ppermute | solution.py:23
  47.6 4.5 %collective-permute-start.8 = (f32[256]{0:T(256)S(1)}, f32[256]{0:T(256)S(1)}, u32[]{:S(2)}, u32[]{:S(2)}) collective-permute-start(f32[256]{0:T(256)S(1)} %add.62), channel_id=1, source_target_pairs={{0,4},{1,5},{2,6},{3,7},{4,0},{5,1},{6,2},{7,3},{8,12},{9,13},{10,... | collective-permute-start | bytes 3080 | tf_op jit(solution)/shard_map/ppermute | solution.py:23
  52.2 7.8 %collective-permute-start.20 = (bf16[256,256]{1,0:T(8,128)(2,1)S(1)}, bf16[256,256]{1,0:T(8,128)(2,1)S(1)}, u32[]{:S(2)}, u32[]{:S(2)}) collective-permute-start(bf16[256,256]{1,0:T(8,128)(2,1)S(1)} %get-tuple-element.51), channel_id=1, source_target_pairs={{0,6},{1,7},{2,4},{3,5},{4,2},{5,3},{6,0},{7,1},{8,14},{9,15},{10,... | collective-permute-start | bytes 393224 | tf_op jit(solution)/shard_map/ppermute | solution.py:23
  55.9 9.1 %collective-permute-start.19 = (bf16[256,256]{1,0:T(8,128)(2,1)S(1)}, bf16[256,256]{1,0:T(8,128)(2,1)S(1)}, u32[]{:S(2)}, u32[]{:S(2)}) collective-permute-start(bf16[256,256]{1,0:T(8,128)(2,1)S(1)} %get-tuple-element.51), channel_id=1, source_target_pairs={{0,4},{1,5},{2,6},{3,7},{4,0},{5,1},{6,2},{7,3},{8,12},{9,13},{10,... | collective-permute-start | bytes 393224 | tf_op jit(solution)/shard_map/ppermute | solution.py:23
  55.9 9.1 %collective-permute-start.18 = (bf16[256,256]{1,0:T(8,128)(2,1)S(1)}, bf16[256,256]{1,0:T(8,128)(2,1)S(1)}, u32[]{:S(2)}, u32[]{:S(2)}) collective-permute-start(bf16[256,256]{1,0:T(8,128)(2,1)S(1)} %get-tuple-element.51), channel_id=1, source_target_pairs={{0,2},{1,3},{2,0},{3,1},{4,6},{5,7},{6,4},{7,5},{8,10},{9,11},{10,... | collective-permute-start | bytes 393224 | tf_op jit(solution)/shard_map/ppermute | solution.py:23
  65.1 6.7 %collective-permute-start.23 = (bf16[256,256]{1,0:T(8,128)(2,1)S(1)}, bf16[256,256]{1,0:T(8,128)(2,1)S(1)}, u32[]{:S(2)}, u32[]{:S(2)}) collective-permute-start(bf16[256,256]{1,0:T(8,128)(2,1)S(1)} %get-tuple-element.43), channel_id=1, source_target_pairs={{0,24},{8,16},{16,8},{24,0},{1,25},{9,17},{17,9},{25,1},{2,26},{10... | collective-permute-start | bytes 393224 | tf_op jit(solution)/shard_map/ppermute | solution.py:23
  67.6 12.3 %collective-permute-start.22 = (bf16[256,256]{1,0:T(8,128)(2,1)S(1)}, bf16[256,256]{1,0:T(8,128)(2,1)S(1)}, u32[]{:S(2)}, u32[]{:S(2)}) collective-permute-start(bf16[256,256]{1,0:T(8,128)(2,1)S(1)} %get-tuple-element.44), channel_id=1, source_target_pairs={{0,16},{8,24},{16,0},{24,8},{1,17},{9,25},{17,1},{25,9},{2,18},{10... | collective-permute-start | bytes 393224 | tf_op jit(solution)/shard_map/ppermute | solution.py:23
  68.1 11.8 %collective-permute-start.21 = (bf16[256,256]{1,0:T(8,128)(2,1)S(1)}, bf16[256,256]{1,0:T(8,128)(2,1)S(1)}, u32[]{:S(2)}, u32[]{:S(2)}) collective-permute-start(bf16[256,256]{1,0:T(8,128)(2,1)S(1)} %get-tuple-element.45), channel_id=1, source_target_pairs={{0,8},{8,0},{16,24},{24,16},{1,9},{9,1},{17,25},{25,17},{2,10},{10... | collective-permute-start | bytes 393224 | tf_op jit(solution)/shard_map/ppermute | solution.py:23
  68.7 14.7 %collective-permute-start.14 = (bf16[512,256]{1,0:T(8,128)(2,1)S(1)}, bf16[512,256]{1,0:T(8,128)(2,1)S(1)}, u32[]{:S(2)}, u32[]{:S(2)}) collective-permute-start(bf16[512,256]{1,0:T(8,128)(2,1)S(1)} %pad_maximum_fusion.4.refs_0_), channel_id=1, source_target_pairs={{0,24},{8,16},{16,8},{24,0},{1,25},{9,17},{17,9},{25,1},{2,26},{10... | collective-permute-start | bytes 786440 | tf_op jit(solution)/shard_map/ppermute | solution.py:23
  71.2 13.5 %collective-permute-start.13 = (bf16[512,256]{1,0:T(8,128)(2,1)S(1)}, bf16[512,256]{1,0:T(8,128)(2,1)S(1)}, u32[]{:S(2)}, u32[]{:S(2)}) collective-permute-start(bf16[512,256]{1,0:T(8,128)(2,1)S(1)} %pad_maximum_fusion.4.refs_0_), channel_id=1, source_target_pairs={{0,16},{8,24},{16,0},{24,8},{1,17},{9,25},{17,1},{25,9},{2,18},{10... | collective-permute-start | bytes 786440 | tf_op jit(solution)/shard_map/ppermute | solution.py:23
  80.0 18.1 %collective-permute-start.24 = (bf16[4,256,256]{2,1,0:T(8,128)(2,1)S(1)}, bf16[4,256,256]{2,1,0:T(8,128)(2,1)S(1)}, u32[]{:S(2)}, u32[]{:S(2)}) collective-permute-start(bf16[4,256,256]{2,1,0:T(8,128)(2,1)S(1)} %pad_maximum_fusion.2), channel_id=1, source_target_pairs={{0,1},{1,0},{2,3},{3,2},{4,5},{5,4},{6,7},{7,6},{8,9},{9,8},{10,11... | collective-permute-start | bytes 1572872 | tf_op jit(solution)/shard_map/ppermute | solution.py:23
  80.0 8.7 %collective-permute-start.12 = (bf16[512,256]{1,0:T(8,128)(2,1)S(1)}, bf16[512,256]{1,0:T(8,128)(2,1)S(1)}, u32[]{:S(2)}, u32[]{:S(2)}) collective-permute-start(bf16[512,256]{1,0:T(8,128)(2,1)S(1)} %pad_maximum_fusion.4.refs_0_), channel_id=1, source_target_pairs={{0,8},{8,0},{16,24},{24,16},{1,9},{9,1},{17,25},{25,17},{2,10},{10... | collective-permute-start | bytes 786440 | tf_op jit(solution)/shard_map/ppermute | solution.py:23
  81.4 9.8 %collective-permute-start.11 = (bf16[256,256]{1,0:T(8,128)(2,1)S(1)}, bf16[256,256]{1,0:T(8,128)(2,1)S(1)}, u32[]{:S(2)}, u32[]{:S(2)}) collective-permute-start(bf16[256,256]{1,0:T(8,128)(2,1)S(1)} %get-tuple-element.33), channel_id=1, source_target_pairs={{0,6},{1,7},{2,4},{3,5},{4,2},{5,3},{6,0},{7,1},{8,14},{9,15},{10,... | collective-permute-start | bytes 393224 | tf_op jit(solution)/shard_map/ppermute | solution.py:23
  83.4 11.0 %collective-permute-start.10 = (bf16[256,256]{1,0:T(8,128)(2,1)S(1)}, bf16[256,256]{1,0:T(8,128)(2,1)S(1)}, u32[]{:S(2)}, u32[]{:S(2)}) collective-permute-start(bf16[256,256]{1,0:T(8,128)(2,1)S(1)} %get-tuple-element.33), channel_id=1, source_target_pairs={{0,4},{1,5},{2,6},{3,7},{4,0},{5,1},{6,2},{7,3},{8,12},{9,13},{10,... | collective-permute-start | bytes 393224 | tf_op jit(solution)/shard_map/ppermute | solution.py:23
  84.6 9.8 %collective-permute-start.9 = (bf16[256,256]{1,0:T(8,128)(2,1)S(1)}, bf16[256,256]{1,0:T(8,128)(2,1)S(1)}, u32[]{:S(2)}, u32[]{:S(2)}) collective-permute-start(bf16[256,256]{1,0:T(8,128)(2,1)S(1)} %get-tuple-element.33), channel_id=1, source_target_pairs={{0,2},{1,3},{2,0},{3,1},{4,6},{5,7},{6,4},{7,5},{8,10},{9,11},{10,... | collective-permute-start | bytes 393224 | tf_op jit(solution)/shard_map/ppermute | solution.py:23
  94.5 11.8 %collective-permute-start.17 = (bf16[256,256]{1,0:T(8,128)(2,1)S(1)}, bf16[256,256]{1,0:T(8,128)(2,1)S(1)}, u32[]{:S(2)}, u32[]{:S(2)}) collective-permute-start(bf16[256,256]{1,0:T(8,128)(2,1)S(1)} %get-tuple-element.47), channel_id=1, source_target_pairs={{0,24},{8,16},{16,8},{24,0},{1,25},{9,17},{17,9},{25,1},{2,26},{10... | collective-permute-start | bytes 393224 | tf_op jit(solution)/shard_map/ppermute | solution.py:23
  96.0 10.3 %collective-permute-start.16 = (bf16[256,256]{1,0:T(8,128)(2,1)S(1)}, bf16[256,256]{1,0:T(8,128)(2,1)S(1)}, u32[]{:S(2)}, u32[]{:S(2)}) collective-permute-start(bf16[256,256]{1,0:T(8,128)(2,1)S(1)} %get-tuple-element.48), channel_id=1, source_target_pairs={{0,16},{8,24},{16,0},{24,8},{1,17},{9,25},{17,1},{25,9},{2,18},{10... | collective-permute-start | bytes 393224 | tf_op jit(solution)/shard_map/ppermute | solution.py:23
  96.8 9.5 %collective-permute-start.15 = (bf16[256,256]{1,0:T(8,128)(2,1)S(1)}, bf16[256,256]{1,0:T(8,128)(2,1)S(1)}, u32[]{:S(2)}, u32[]{:S(2)}) collective-permute-start(bf16[256,256]{1,0:T(8,128)(2,1)S(1)} %get-tuple-element.49), channel_id=1, source_target_pairs={{0,8},{8,0},{16,24},{24,16},{1,9},{9,1},{17,25},{25,17},{2,10},{10... | collective-permute-start | bytes 393224 | tf_op jit(solution)/shard_map/ppermute | solution.py:23
  106.4 2.0 %collective-permute-start.25 = (bf16[4,256,256]{2,1,0:T(8,128)(2,1)S(1)}, bf16[4,256,256]{2,1,0:T(8,128)(2,1)S(1)}, u32[]{:S(2)}, u32[]{:S(2)}) collective-permute-start(bf16[4,256,256]{2,1,0:T(8,128)(2,1)S(1)} %pad_maximum_fusion.3), channel_id=1, source_target_pairs={{0,1},{1,0},{2,3},{3,2},{4,5},{5,4},{6,7},{7,6},{8,9},{9,8},{10,11... | collective-permute-start | bytes 1572872 | tf_op jit(solution)/shard_map/ppermute | solution.py:23
